TPU v7x, 256 devices: a whole 4x4x8 slice. The times are simulated.
256 devices in a mesh: rep: 16 (over y_lo, z), tp: 16 (over x, y_hi, core).
Axes of the slice: x: 4, y: 4 (y_hi: 2, y_lo: 2; y = y_hi * 2 + y_lo), z: 8, core: 2. Of those that a mesh axis runs over, the one named last changes fastest.
Arguments:
- tokens: bfloat16 [16384, 8192], P('rep', 'tp'), may hold values from -6 to 6
- grad_out: bfloat16 [16384, 4096], P('rep', 'tp'), may hold values from -0.046875 to 0.046875
- lengths: int32 [16, 16], replicated, may hold values from 0 to 256, as said below
- master: float32 [8192, 2048], P('rep', 'tp'), may hold values from -3 to 3
- first: float32 [8192, 2048], P('rep', 'tp'), may hold values from -6 to 6
- second: float32 [8192, 2048], P('rep', 'tp'), may hold values from 0.25 to 4
Outputs:
- new_master: float32 [8192, 2048], P('rep', 'tp')
- new_first: float32 [8192, 2048], P('rep', 'tp')
- new_second: float32 [8192, 2048], P('rep', 'tp')
- healthy_weights: bfloat16 [8192, 2048], P(None, 'tp')
- slot_weights: bfloat16 [16, 8192, 4096], P('rep', None, 'tp')
Inputs may be any that keep to these rules, and one draw needn't show every extreme that they name: `lengths`: each row is one replica's split of the 2048 columns over its devices in tp order: the entries are multiples of 64, sum to 2048, the nonzero ones come first and number at least half of the row; a row is either all 128 or has an entry equal to 256, and some row has an entry equal to 256.
All inputs are finite; a program needn't handle non-finite values.
Results may differ from a plain program's by a relative error of at most 0.0019.
Values may be sent and summed in bfloat16 or wider, within the bound.
No kernel may reach another device: no remote copies, remote signals or barrier semaphores. Data moves between devices by JAX's collectives and lax.ppermute only.
A program may use at most 128 MiB of HBM per device.

v0:
```python
import jax
import jax.numpy as jnp
from jax import lax
from jax.sharding import Mesh
from jax.sharding import PartitionSpec as P

COLS = 2048
STEP = 1000
REP = ("rep_0", "rep_1")
decay_first = 0.9
decay_second = 0.999
learning_rate = 0.02
weight_decay = 0.1
epsilon = 1e-08


def own_block(parts, axes, turns):
    inside = parts.shape[1:]
    parts = parts.reshape(*(lax.axis_size(a) for a in axes), *inside)
    parts = jnp.moveaxis(parts, turns, range(len(axes))).reshape(-1, *inside)
    for k in turns:
        parts = lax.psum_scatter(parts, axes[k], scatter_dimension=0, tiled=True)
    return parts[0]


def in_blocks(value, dim, size):
    before, after = (value.shape[:dim], value.shape[dim + 1 :])
    return jnp.moveaxis(value.reshape(*before, size, -1, *after), dim, 0)


def summed_rows(value, axes, turns, dim):
    size = lax.axis_size(axes)
    return own_block(in_blocks(value, dim, size), axes, turns)


def from_everyone(value, axis):
    copies = jnp.broadcast_to(value, (lax.axis_size(axis), *value.shape))
    return lax.all_to_all(copies, axis, split_axis=0, concat_axis=0, tiled=True)


def laid_out(parts, dim):
    shape = list(parts.shape[1:])
    shape[dim] *= parts.shape[0]
    return jnp.moveaxis(parts, 0, dim).reshape(shape)


def gathered_copies(value, axis, dim):
    parts = from_everyone(value, axis)
    return laid_out(parts, dim)


def adam_update(master, first, second, gradient):
    scale_first = 1.0 - decay_first**STEP
    scale_second = 1.0 - decay_second**STEP
    new_first = decay_first * first + (1.0 - decay_first) * gradient
    new_second = decay_second * second + (1.0 - decay_second) * gradient * gradient
    direction = new_first / scale_first / (jnp.sqrt(new_second / scale_second) + epsilon)
    new_master = master - learning_rate * (direction + weight_decay * master)
    return (new_master, new_first, new_second)


def on_device(tokens, grad_out, lengths, master, first, second):
    shards = lax.axis_size("tp")
    replicas = lax.axis_size(REP)
    column_index = lax.axis_index("tp")
    replica_index = lax.axis_index(REP)
    token_count = tokens.shape[0]
    slot_width = grad_out.shape[1]
    block_width = COLS // shards
    begins_all = jnp.cumsum(lengths, axis=1) - lengths
    is_mine = jnp.arange(shards, dtype=jnp.int32) == column_index
    own_lengths = lax.dynamic_index_in_dim(lengths, replica_index, 0, keepdims=False)
    own_begins = lax.dynamic_index_in_dim(begins_all, replica_index, 0, keepdims=False)
    my_begin = jnp.sum(jnp.where(is_mine, own_begins, 0))
    my_length = jnp.sum(jnp.where(is_mine, own_lengths, 0))
    columns = jnp.arange(COLS, dtype=jnp.int32)
    offset = columns - my_begin
    inside = (offset >= 0) & (offset < my_length)
    picked = jnp.take(grad_out, jnp.clip(offset, 0, slot_width - 1), axis=1)
    spread = jnp.where(inside[None, :], picked, jnp.zeros_like(picked)).reshape(
        token_count, shards, block_width
    )
    received = lax.all_to_all(spread, "tp", split_axis=1, concat_axis=1, tiled=True)
    grad_block = jnp.sum(received, axis=1)
    grad_columns = lax.dot_general(
        lax.all_gather(tokens, "tp", axis=1, tiled=True),
        grad_block,
        (((0,), (0,)), ((), ())),
        preferred_element_type=jnp.float32,
    )
    summed = summed_rows(grad_columns.astype(jnp.bfloat16), REP, (1, 0), 0).astype(jnp.float32)
    new_master, new_first, new_second = adam_update(master, first, second, summed)
    weights = new_master.astype(jnp.bfloat16)
    healthy = gathered_copies(weights, REP, 0)
    replica_rows = lax.all_gather(weights, "tp", axis=1, tiled=True)
    slot_begins = jnp.sum(jnp.where(is_mine[None, :], begins_all, 0), axis=1)
    slot_lengths = jnp.sum(jnp.where(is_mine[None, :], lengths, 0), axis=1)
    within = jnp.arange(slot_width, dtype=jnp.int32)
    source_cols = slot_begins[:, None] + within[None, :]
    valid = within[None, :] < slot_lengths[:, None]
    taken = jnp.take(replica_rows, jnp.clip(source_cols, 0, COLS - 1).reshape(-1), axis=1)
    outgoing = jnp.where(valid.reshape(-1)[None, :], taken, jnp.zeros_like(taken))
    outgoing = outgoing.reshape(replica_rows.shape[0], replicas, slot_width)
    arrived = lax.all_to_all(outgoing, REP, split_axis=1, concat_axis=0, tiled=True)
    slot_weights = arrived.reshape(1, -1, slot_width)
    return (new_master, new_first, new_second, healthy, slot_weights)


def solution(mesh):
    torus = Mesh(mesh.devices.reshape(2, 8, mesh.shape["tp"]), ("rep_0", "rep_1", "tp"))
    placed = (P(REP, "tp"), P(REP, "tp"), P(), P(REP, "tp"), P(REP, "tp"), P(REP, "tp"))
    return jax.shard_map(
        on_device,
        mesh=torus,
        in_specs=placed,
        out_specs=(P(REP, "tp"), P(REP, "tp"), P(REP, "tp"), P(None, "tp"), P(REP, None, "tp")),
        check_vma=False,
    )
```

profile of v0, /device:TPU:32, one launch (start us, length us, event | category | flops | bytes accessed | tf_op | source)
XLA Modules:
  0.0 450.8 jit_solution(10688095374911271748)
XLA Ops:
  8.0 0.9 reduce_window_sum.11
  8.8 1.2 copy.34
  10.9 1.3 fusion.12
  12.9 9.6 %gather_fusion = bf16[2048,1024]{1,0:T(8,128)(2,1)} fusion(bf16[1024,256]{0,1:T(8,128)(2,1)S(1)} %copy.34, s32[2048]{0:T(1024)S(1)} %broadcast_clamp_fusion.1), kind=kCustom, calls=%fused_computation | custom fusion | bytes 8396800 | tf_op jit(solution)/shard_map/jit(_take)/gather | solution.py:79
  23.2 1.3 fusion.11
  24.5 3.1 select_select_fusion.1
  27.6 73.9 %all_to_all.25 = bf16[1024,16,128]{0,2,1:T(8,128)(2,1)} all-to-all(bf16[1024,16,128]{0,2,1:T(8,128)(2,1)S(1)} %select_select_fusion.1), channel_id=1, replica_groups=mesh['rep_0'=2,'rep_1'=8,'tp'=16] {'tp'}, dimensions={1} | all-to-all | bytes 8388608 | tf_op jit(solution)/shard_map/all_to_all | solution.py:83
  101.5 3.1 reduce_sum.50
  104.7 63.9 %all-gather.3.cloned.1.call-done = bf16[1024,8192]{1,0:T(8,128)(2,1)} async-done(((bf16[1024,512]{1,0:T(8,128)(2,1)}), bf16[1024,8192]{1,0:T(8,128)(2,1)}) %all-gather.3.cloned.1.call-update) | async-done | bytes 16777232 | tf_op jit(solution)/shard_map/all_gather | solution.py:86
  168.6 8.1 %convolution_convert_fusion = bf16[128,8192]{1,0:T(8,128)(2,1)S(1)} fusion(bf16[1024,128]{0,1:T(8,128)(2,1)S(1)} %reduce_sum.50, bf16[1024,8192]{1,0:T(8,128)(2,1)} %all-gather.3.cloned.1.call-done), kind=kOutput, calls=%fused_computation.2 | convolution fusion | flops 2148532224 | bytes 19136512 | tf_op jit(solution)/shard_map/dot_general | solution.py:85
  177.6 2.5 copy.35
  180.2 41.0 %reduce-scatter.3.cloned.1.call-done = bf16[2,512,128]{1,2,0:T(8,128)(2,1)} async-done(((bf16[16,512,128]{1,2,0:T(8,128)(2,1)}), bf16[2,512,128]{1,2,0:T(8,128)(2,1)}) %reduce-scatter.3.cloned.1.call-update) | async-done | bytes 262160 | tf_op jit(solution)/shard_map/reduce_scatter | solution.py:22
  221.7 18.0 %reduce-scatter.5.cloned.1.call-done = bf16[1,512,128]{1,2,0:T(8,128)(2,1)} async-done(((bf16[2,512,128]{1,2,0:T(8,128)(2,1)}), bf16[1,512,128]{1,2,0:T(8,128)(2,1)}) %reduce-scatter.5.cloned.1.call-update) | async-done | bytes 131088 | tf_op jit(solution)/shard_map/reduce_scatter | solution.py:22
  239.7 1.8 fusion.14
  241.5 1.0 copy.39
  242.5 1.7 broadcast_in_dim.78
  244.3 7.5 %all-to-all-start.1 = ((bf16[16,512,128]{2,1,0:T(8,128)(2,1)}), bf16[16,512,128]{2,1,0:T(8,128)(2,1)S(1)}, u32[]{:S(2)}, u32[]{:S(2)}) async-start(bf16[16,512,128]{2,1,0:T(8,128)(2,1)} %broadcast_in_dim.78), calls=%async_computation.3 | async-start | bytes 4194304 | tf_op jit(solution)/shard_map/all_to_all | solution.py:38
  252.0 52.9 %all-gather.5.cloned.1.call-done = bf16[512,2048]{0,1:T(8,128)(2,1)} async-done(((bf16[512,128]{0,1:T(8,128)(2,1)}), bf16[512,2048]{0,1:T(8,128)(2,1)}) %all-gather.5.cloned.1.call-update) | async-done | bytes 2097168 | tf_op jit(solution)/shard_map/all_gather | solution.py:95
  304.9 19.3 %gather_fusion.1 = bf16[4096,512]{1,0:T(8,128)(2,1)} fusion(bf16[512,2048]{0,1:T(8,128)(2,1)} %all-gather.5.cloned.1.call-done, s32[4096]{0:T(1024)S(1)} %broadcast_clamp_fusion), kind=kCustom, calls=%fused_computation.1 | custom fusion | bytes 8404992 | tf_op jit(solution)/shard_map/jit(_take)/gather | solution.py:101
  324.2 5.2 %select_select_fusion = bf16[512,16,256]{0,2,1:T(8,128)(2,1)} fusion(bf16[512,16,256]{0,2,1:T(8,128)(2,1)} %bitcast.43, pred[16,256]{1,0:T(8,128)(4,1)S(1)} %get-tuple-element.30, pred[16,256]{1,0:T(8,128)(4,1)S(1)} %get-tuple-element.29), kind=kLoop, calls=%fused_computation.3 | loop fusion | flops 4194304 | bytes 8396800 | tf_op jit(solution)/shard_map/jit(_where)/select_n | solution.py:102
  329.5 11.3 %all-to-all-start.2 = ((bf16[512,16,256]{0,2,1:T(8,128)(2,1)}), bf16[512,16,256]{0,2,1:T(8,128)(2,1)}, u32[]{:S(2)}, u32[]{:S(2)}) async-start(bf16[512,16,256]{0,2,1:T(8,128)(2,1)} %select_select_fusion), calls=%async_computation.4 | async-start | bytes 8388608 | tf_op jit(solution)/shard_map/all_to_all | solution.py:104
  343.2 93.3 %all-to-all-done.2 = bf16[512,16,256]{0,2,1:T(8,128)(2,1)} async-done(((bf16[512,16,256]{0,2,1:T(8,128)(2,1)}), bf16[512,16,256]{0,2,1:T(8,128)(2,1)}, u32[]{:S(2)}, u32[]{:S(2)}) %all-to-all-start.2) | async-done | bytes 4194336 | tf_op jit(solution)/shard_map/all_to_all | solution.py:104
  436.6 6.4 %copy.40 = bf16[16,512,1,256]{3,1,0,2:T(8,128)(2,1)} copy(bf16[16,512,1,256]{1,3,0,2:T(8,128)(2,1)} %bitcast.15) | data formatting | bytes 8388608 | tf_op jit(solution)/shard_map/all_to_all | solution.py:104
  443.0 1.3 copy.47
  (32 shorter events, 7.0 us)
Async XLA Ops:
  7.2 161.4 %all-gather.3.cloned.1.call-start = ((), (), s32[]{:S(2)}) async-start(), calls=%async_computation.5 | async-start | bytes 17825792 | tf_op jit(solution)/shard_map/all_gather | solution.py:86
  7.9 213.3 %reduce-scatter.3.cloned.1.call-start = ((), (), s32[]{:S(2)}) async-start(), calls=%async_computation.6 | async-start | bytes 2359296 | tf_op jit(solution)/shard_map/reduce_scatter | solution.py:22
  177.6 43.7 %copy-start = (f32[512,128]{1,0:T(8,128)S(1)}, f32[512,128]{1,0:T(8,128)}, u32[]{:S(2)}) copy-start(f32[512,128]{1,0:T(8,128)} %param.10) | copy-start | bytes 786436
  177.6 43.8 %copy-start.1 = (f32[512,128]{1,0:T(8,128)S(1)}, f32[512,128]{1,0:T(8,128)}, u32[]{:S(2)}) copy-start(f32[512,128]{1,0:T(8,128)} %param.11) | copy-start | bytes 786436
  177.6 43.9 %copy-start.2 = (f32[512,128]{1,0:T(8,128)S(1)}, f32[512,128]{1,0:T(8,128)}, u32[]{:S(2)}) copy-start(f32[512,128]{1,0:T(8,128)} %param.9) | copy-start | bytes 786436
  180.1 59.6 %reduce-scatter.5.cloned.1.call-start = ((), (), s32[]{:S(2)}) async-start(), calls=%async_computation.7 | async-start | bytes 393216 | tf_op jit(solution)/shard_map/reduce_scatter | solution.py:22
  221.2 83.7 %all-gather.5.cloned.1.call-start = ((), (), s32[]{:S(2)}) async-start(), calls=%async_computation.8 | async-start | bytes 2228224 | tf_op jit(solution)/shard_map/all_gather | solution.py:95
  244.3 85.2 %all-to-all-start.1 = ((bf16[16,512,128]{2,1,0:T(8,128)(2,1)}), bf16[16,512,128]{2,1,0:T(8,128)(2,1)S(1)}, u32[]{:S(2)}, u32[]{:S(2)}) async-start(bf16[16,512,128]{2,1,0:T(8,128)(2,1)} %broadcast_in_dim.78), calls=%async_computation.3 | async-start | bytes 4194304 | tf_op jit(solution)/shard_map/all_to_all | solution.py:38
  329.5 107.1 %all-to-all-start.2 = ((bf16[512,16,256]{0,2,1:T(8,128)(2,1)}), bf16[512,16,256]{0,2,1:T(8,128)(2,1)}, u32[]{:S(2)}, u32[]{:S(2)}) async-start(bf16[512,16,256]{0,2,1:T(8,128)(2,1)} %select_select_fusion), calls=%async_computation.4 | async-start | bytes 8388608 | tf_op jit(solution)/shard_map/all_to_all | solution.py:104
Sparse Core Ops, SparseCore 0:
  10.5 158.0 all-gather.2
  180.3 40.8 reduce-scatter.2
  223.7 16.0 reduce-scatter.4
  242.8 62.0 all-gather.4
where the time goes:
time: 452 us; the launch traced here: 451 us
  waiting for transfers between devices  270 us (60%)
  blocking collectives  73.9 us (16%)
  local copies, waits for them, and re-layouts  46.9 us (10%)
  other arithmetic  19.1 us (4%)
  starting transfers between devices  18.9 us (4%)
  between operations  13.9 us (3%)
  matrix products  8.12 us (2%)
    all_to_all x1, waiting for transfers between devices, on_device(): lax.all_to_all(outgoing, REP, split_axis=1, concat_axis=0, tiled=True)  93.3 us
    all_to_all x1, blocking collectives, on_device(): lax.all_to_all(spread, 'tp', split_axis=1, concat_axis=1, tiled=True)  73.9 us
    all_gather x1, waiting for transfers between devices, on_device(): lax.all_gather(tokens, 'tp', axis=1, tiled=True)  63.9 us
    reduce_scatter x2, waiting for transfers between devices, own_block(): parts = lax.psum_scatter(parts, axes[k], scatter_dimension=0, tiled=True)  59 us
    all_gather x1, waiting for transfers between devices, on_device(): replica_rows = lax.all_gather(weights, 'tp', axis=1, tiled=True)  52.9 us
    gather x1, local copies, waits for them, and re-layouts, on_device(): jnp.take(replica_rows, jnp.clip(source_cols, 0, COLS - 1).reshape(-1), ax...  19.3 us
    all_to_all x1, starting transfers between devices, on_device(): lax.all_to_all(outgoing, REP, split_axis=1, concat_axis=0, tiled=True)  11.3 us
    gather x1, local copies, waits for them, and re-layouts, on_device(): picked = jnp.take(grad_out, jnp.clip(offset, 0, slot_width - 1), axis=1)  9.61 us
  transfers between devices with their start and end apart: 6, of which 5 were waited for; matrix products, arithmetic and copies ran while one was open for 12% of the time, Pallas kernels for 0%

commit v1 on v0

--- a/solution.py
+++ b/solution.py
@@ -12,6 +12,12 @@
 learning_rate = 0.02
 weight_decay = 0.1
 epsilon = 1e-08
+
+
+def gather_blocks(x, name, dim):
+    blocks = lax.all_gather(x, name, axis=0, tiled=False)
+    result = jnp.concatenate(blocks, axis=dim)
+    return result
 
 
 def own_block(parts, axes, turns):
@@ -83,7 +89,7 @@
     received = lax.all_to_all(spread, "tp", split_axis=1, concat_axis=1, tiled=True)
     grad_block = jnp.sum(received, axis=1)
     grad_columns = lax.dot_general(
-        lax.all_gather(tokens, "tp", axis=1, tiled=True),
+        gather_blocks(tokens, "tp", 1),
         grad_block,
         (((0,), (0,)), ((), ())),
         preferred_element_type=jnp.float32,

time: 452 us -> 464 us (1.027)
  local copies, waits for them, and re-layouts: 46.9 us -> 68.6 us
  waiting for transfers between devices: 270 us -> 258 us
    reshape x0 -> x1, local copies, waits for them, and re-layouts: none -> 21.7 us  [gather_blocks(): result = jnp.concatenate(blocks, axis=dim)]
    all_gather x1, waiting for transfers between devices: 63.9 us -> 52.1 us  [gather_blocks(): blocks = lax.all_gather(x, name, axis=0, tiled=False)]
  transfers between devices with their start and end apart: 6 -> 6, of which waited for: 5 -> 5; matrix products, arithmetic and copies ran while one was open for 12% -> 11% of each run, Pallas kernels for 0% -> 0%
where the time goes in v1:
time: 464 us; the launch traced here: 463 us
  waiting for transfers between devices  258 us (56%)
  blocking collectives  72.6 us (16%)
  local copies, waits for them, and re-layouts  68.6 us (15%)
  other arithmetic  19.1 us (4%)
  starting transfers between devices  18.9 us (4%)
  between operations  13.9 us (3%)
  matrix products  11.3 us (2%)
    all_to_all x1, waiting for transfers between devices, on_device(): lax.all_to_all(outgoing, REP, split_axis=1, concat_axis=0, tiled=True)  93.3 us
    all_to_all x1, blocking collectives, on_device(): lax.all_to_all(spread, 'tp', split_axis=1, concat_axis=1, tiled=True)  72.6 us
    reduce_scatter x2, waiting for transfers between devices, own_block(): parts = lax.psum_scatter(parts, axes[k], scatter_dimension=0, tiled=True)  59 us
    all_gather x1, waiting for transfers between devices, on_device(): replica_rows = lax.all_gather(weights, 'tp', axis=1, tiled=True)  53 us
    all_gather x1, waiting for transfers between devices, gather_blocks(): blocks = lax.all_gather(x, name, axis=0, tiled=False)  52.1 us
    reshape x1, local copies, waits for them, and re-layouts, gather_blocks(): result = jnp.concatenate(blocks, axis=dim)  21.7 us
    gather x1, local copies, waits for them, and re-layouts, on_device(): jnp.take(replica_rows, jnp.clip(source_cols, 0, COLS - 1).reshape(-1), ax...  19.3 us
    dot_general x1, matrix products, on_device(): lax.dot_general(gather_blocks(tokens, 'tp', 1), grad_block, (((0,), (0,))...  11.3 us
  transfers between devices with their start and end apart: 6, of which 5 were waited for; matrix products, arithmetic and copies ran while one was open for 11% of the time, Pallas kernels for 0%

profile of v1, /device:TPU:32, one launch (start us, length us, event | category | flops | bytes accessed | tf_op | source)
XLA Modules:
  0.0 462.5 jit_solution(2251249999387566332)
XLA Ops:
  8.8 1.2 copy.46
  10.9 1.3 fusion.12
  12.9 9.6 %gather_fusion = bf16[2048,1024]{1,0:T(8,128)(2,1)} fusion(bf16[1024,256]{0,1:T(8,128)(2,1)S(1)} %copy.46, s32[2048]{0:T(1024)S(1)} %broadcast_clamp_fusion.1), kind=kCustom, calls=%fused_computation | custom fusion | bytes 8396800 | tf_op jit(solution)/shard_map/jit(_take)/gather | solution.py:85
  23.2 1.3 fusion.11
  24.5 3.1 select_select_fusion.1
  27.6 72.6 %all_to_all.25 = bf16[1024,16,128]{0,2,1:T(8,128)(2,1)} all-to-all(bf16[1024,16,128]{0,2,1:T(8,128)(2,1)S(1)} %select_select_fusion.1), channel_id=1, replica_groups=mesh['rep_0'=2,'rep_1'=8,'tp'=16] {'tp'}, dimensions={1} | all-to-all | bytes 8388608 | tf_op jit(solution)/shard_map/all_to_all | solution.py:89
  100.2 3.1 reduce_sum.50
  103.3 52.1 %all-gather.6.cloned.1.call-done = bf16[16384,512]{1,0:T(8,128)(2,1)} async-done(((bf16[1024,512]{1,0:T(8,128)(2,1)}), bf16[16384,512]{1,0:T(8,128)(2,1)}) %all-gather.6.cloned.1.call-update) | async-done | bytes 16777232 | tf_op jit(solution)/shard_map/all_gather | solution.py:18
  155.4 21.7 %copy.47 = bf16[1024,16,512]{0,2,1:T(8,128)(2,1)} copy(bf16[1024,16,512]{2,0,1:T(8,128)(2,1)} %bitcast.50) | data formatting | bytes 33554432 | tf_op jit(solution)/shard_map/reshape | solution.py:19
  177.1 11.3 %convolution_convert_fusion = bf16[128,8192]{1,0:T(8,128)(2,1)S(1)} fusion(bf16[1024,128]{0,1:T(8,128)(2,1)S(1)} %reduce_sum.50, bf16[1024,8192]{0,1:T(8,128)(2,1)} %bitcast.47), kind=kOutput, calls=%fused_computation.2 | convolution fusion | flops 2148532224 | bytes 19136512 | tf_op jit(solution)/shard_map/dot_general | solution.py:91
  189.3 2.5 copy.48
  191.9 40.9 %reduce-scatter.3.cloned.1.call-done = bf16[2,512,128]{1,2,0:T(8,128)(2,1)} async-done(((bf16[16,512,128]{1,2,0:T(8,128)(2,1)}), bf16[2,512,128]{1,2,0:T(8,128)(2,1)}) %reduce-scatter.3.cloned.1.call-update) | async-done | bytes 262160 | tf_op jit(solution)/shard_map/reduce_scatter | solution.py:28
  233.3 18.1 %reduce-scatter.5.cloned.1.call-done = bf16[1,512,128]{1,2,0:T(8,128)(2,1)} async-done(((bf16[2,512,128]{1,2,0:T(8,128)(2,1)}), bf16[1,512,128]{1,2,0:T(8,128)(2,1)}) %reduce-scatter.5.cloned.1.call-update) | async-done | bytes 131088 | tf_op jit(solution)/shard_map/reduce_scatter | solution.py:28
  251.4 1.8 fusion.14
  253.2 1.0 copy.52
  254.2 1.7 broadcast_in_dim.78
  256.0 7.5 %all-to-all-start.1 = ((bf16[16,512,128]{2,1,0:T(8,128)(2,1)}), bf16[16,512,128]{2,1,0:T(8,128)(2,1)S(1)}, u32[]{:S(2)}, u32[]{:S(2)}) async-start(bf16[16,512,128]{2,1,0:T(8,128)(2,1)} %broadcast_in_dim.78), calls=%async_computation.3 | async-start | bytes 4194304 | tf_op jit(solution)/shard_map/all_to_all | solution.py:44
  263.7 53.0 %all-gather.4.cloned.1.call-done = bf16[512,2048]{0,1:T(8,128)(2,1)} async-done(((bf16[512,128]{0,1:T(8,128)(2,1)}), bf16[512,2048]{0,1:T(8,128)(2,1)}) %all-gather.4.cloned.1.call-update) | async-done | bytes 2097168 | tf_op jit(solution)/shard_map/all_gather | solution.py:101
  316.7 19.3 %gather_fusion.1 = bf16[4096,512]{1,0:T(8,128)(2,1)} fusion(bf16[512,2048]{0,1:T(8,128)(2,1)} %all-gather.4.cloned.1.call-done, s32[4096]{0:T(1024)S(1)} %broadcast_clamp_fusion), kind=kCustom, calls=%fused_computation.1 | custom fusion | bytes 8404992 | tf_op jit(solution)/shard_map/jit(_take)/gather | solution.py:107
  336.0 5.2 %select_select_fusion = bf16[512,16,256]{0,2,1:T(8,128)(2,1)} fusion(bf16[512,16,256]{0,2,1:T(8,128)(2,1)} %bitcast.48, pred[16,256]{1,0:T(8,128)(4,1)S(1)} %get-tuple-element.35, pred[16,256]{1,0:T(8,128)(4,1)S(1)} %get-tuple-element.34), kind=kLoop, calls=%fused_computation.3 | loop fusion | flops 4194304 | bytes 8396800 | tf_op jit(solution)/shard_map/jit(_where)/select_n | solution.py:108
  341.2 11.2 %all-to-all-start.2 = ((bf16[512,16,256]{0,2,1:T(8,128)(2,1)}), bf16[512,16,256]{0,2,1:T(8,128)(2,1)}, u32[]{:S(2)}, u32[]{:S(2)}) async-start(bf16[512,16,256]{0,2,1:T(8,128)(2,1)} %select_select_fusion), calls=%async_computation.4 | async-start | bytes 8388608 | tf_op jit(solution)/shard_map/all_to_all | solution.py:110
  354.9 93.3 %all-to-all-done.2 = bf16[512,16,256]{0,2,1:T(8,128)(2,1)} async-done(((bf16[512,16,256]{0,2,1:T(8,128)(2,1)}), bf16[512,16,256]{0,2,1:T(8,128)(2,1)}, u32[]{:S(2)}, u32[]{:S(2)}) %all-to-all-start.2) | async-done | bytes 4194336 | tf_op jit(solution)/shard_map/all_to_all | solution.py:110
  448.3 6.4 %copy.53 = bf16[16,512,1,256]{3,1,0,2:T(8,128)(2,1)} copy(bf16[16,512,1,256]{1,3,0,2:T(8,128)(2,1)} %bitcast.18) | data formatting | bytes 8388608 | tf_op jit(solution)/shard_map/all_to_all | solution.py:110
  454.7 1.3 copy.60
  (33 shorter events, 7.8 us)
Async XLA Ops:
  7.2 148.3 %all-gather.6.cloned.1.call-start = ((), (), s32[]{:S(2)}) async-start(), calls=%async_computation.8 | async-start | bytes 17825792 | tf_op jit(solution)/shard_map/all_gather | solution.py:18
  7.9 224.9 %reduce-scatter.3.cloned.1.call-start = ((), (), s32[]{:S(2)}) async-start(), calls=%async_computation.5 | async-start | bytes 2359296 | tf_op jit(solution)/shard_map/reduce_scatter | solution.py:28
  189.3 43.6 %copy-start = (f32[512,128]{1,0:T(8,128)S(1)}, f32[512,128]{1,0:T(8,128)}, u32[]{:S(2)}) copy-start(f32[512,128]{1,0:T(8,128)} %param.9) | copy-start | bytes 786436
  189.3 43.7 %copy-start.1 = (f32[512,128]{1,0:T(8,128)S(1)}, f32[512,128]{1,0:T(8,128)}, u32[]{:S(2)}) copy-start(f32[512,128]{1,0:T(8,128)} %param.10) | copy-start | bytes 786436
  189.3 43.8 %copy-start.2 = (f32[512,128]{1,0:T(8,128)S(1)}, f32[512,128]{1,0:T(8,128)}, u32[]{:S(2)}) copy-start(f32[512,128]{1,0:T(8,128)} %param.11) | copy-start | bytes 786436
  191.8 59.6 %reduce-scatter.5.cloned.1.call-start = ((), (), s32[]{:S(2)}) async-start(), calls=%async_computation.6 | async-start | bytes 393216 | tf_op jit(solution)/shard_map/reduce_scatter | solution.py:28
  232.8 83.8 %all-gather.4.cloned.1.call-start = ((), (), s32[]{:S(2)}) async-start(), calls=%async_computation.7 | async-start | bytes 2228224 | tf_op jit(solution)/shard_map/all_gather | solution.py:101
  256.0 85.2 %all-to-all-start.1 = ((bf16[16,512,128]{2,1,0:T(8,128)(2,1)}), bf16[16,512,128]{2,1,0:T(8,128)(2,1)S(1)}, u32[]{:S(2)}, u32[]{:S(2)}) async-start(bf16[16,512,128]{2,1,0:T(8,128)(2,1)} %broadcast_in_dim.78), calls=%async_computation.3 | async-start | bytes 4194304 | tf_op jit(solution)/shard_map/all_to_all | solution.py:44
  341.2 107.1 %all-to-all-start.2 = ((bf16[512,16,256]{0,2,1:T(8,128)(2,1)}), bf16[512,16,256]{0,2,1:T(8,128)(2,1)}, u32[]{:S(2)}, u32[]{:S(2)}) async-start(bf16[512,16,256]{0,2,1:T(8,128)(2,1)} %select_select_fusion), calls=%async_computation.4 | async-start | bytes 8388608 | tf_op jit(solution)/shard_map/all_to_all | solution.py:110
Sparse Core Ops, SparseCore 0:
  10.7 144.7 all-gather.5
  192.0 40.7 reduce-scatter.2
  235.3 16.0 reduce-scatter.4
  254.5 62.0 all-gather.3
